TPU v7x, 512 devices: a whole 4x4x16 slice. The times are simulated.
512 devices in a mesh: layer: 32 (over x, z_lo), dp: 16 (over y, z_hi, core).
Axes of the slice: x: 4, y: 4, z: 16 (z_hi: 2, z_lo: 8; z = z_hi * 8 + z_lo), core: 2. Of those that a mesh axis runs over, the one named last changes fastest.
Arguments:
- activations: bfloat16 [32, 10240, 2048], P('layer', 'dp'), may hold values from -6 to 6
- out_grads: bfloat16 [32, 10240, 512], P('layer', 'dp'), may hold values from -0.059814453 to 0.059814453
- a_inverse: bfloat16 [32, 2048, 2048], P('layer', 'dp'), may hold values from -1 to 3, as said below
- s_inverse: bfloat16 [32, 512, 512], P('layer'), may hold values from -1 to 3, as said below
- in_decay: float32 [32, 2048], P('layer', 'dp'), may hold values from 0 to 1
- out_decay: float32 [32, 512], P('layer'), may hold values from 0 to 1
Outputs:
- direction: bfloat16 [32, 2048, 512], P('layer', 'dp')
Inputs may be any that keep to these rules, and one draw needn't show every extreme that they name: `a_inverse`: each layer's matrix is a positive diagonal plus dense small entries. `s_inverse`: each layer's matrix is a positive diagonal plus dense small entries.
All inputs are finite; a program needn't handle non-finite values.
Results may differ from a plain program's by a relative error of at most 0.0036.
Values may be sent and summed in bfloat16 or wider, within the bound.
A program may use at most 64 MiB of HBM per device.

v0:
```python
import jax
import jax.numpy as jnp
from jax import lax
from jax.sharding import PartitionSpec as P


def prefix(shard, axis, combine, identity, reverse):
    peers, here = (lax.axis_size(axis), lax.axis_index(axis))
    everything = jax.tree.map(lambda part: lax.all_gather(part, axis), shard)
    start = jax.tree.map(
        lambda part, zero: jnp.broadcast_to(jnp.asarray(zero, part.dtype), part.shape),
        shard,
        identity,
    )

    def turn(k, before):
        at = peers - 1 - k if reverse else k
        reached = at > here if reverse else at < here
        new = combine(before, jax.tree.map(lambda part: part[at], everything))
        return jax.tree.map(lambda a, b: jnp.where(reached, a, b), new, before)

    return lax.fori_loop(0, peers, turn, start)


def compose(earlier, later):
    joined = later[2] + later[0][:, None] * later[1][None, :] * earlier[2]
    return (later[0] * earlier[0], later[1] * earlier[1], joined)


def shards(activations, out_grads, a_inverse, s_inverse, in_decay, out_decay):
    inputs_here = activations[0]
    grads_here = out_grads[0]
    row_count = a_inverse.shape[1]
    contract = (((0,), (0,)), ((), ()))
    partial_full = lax.dot_general(
        inputs_here, grads_here, contract, preferred_element_type=jnp.float32
    )
    summed = lax.psum(partial_full, "dp")
    grad_rows = lax.dynamic_slice_in_dim(summed, lax.axis_index("dp") * row_count, row_count, 0)
    rates_in = in_decay[0]
    rates_out = out_decay[0]
    coupling = rates_in[:, None] * rates_out[None, :]
    identity = (jnp.ones_like(rates_in), jnp.ones_like(rates_out), jnp.zeros_like(grad_rows))
    later_solved = prefix((rates_in, rates_out, grad_rows), "layer", compose, identity, True)[2]
    upper_solved = grad_rows + coupling * later_solved
    s_applied = jnp.dot(
        upper_solved.astype(jnp.bfloat16), s_inverse[0], preferred_element_type=jnp.float32
    ).astype(jnp.bfloat16)
    a_rows = a_inverse[0]
    solved = jnp.dot(
        a_rows,
        lax.all_gather(s_applied, "dp", axis=0, tiled=True),
        preferred_element_type=jnp.float32,
    )
    earlier_state = prefix(
        (rates_in, rates_out, coupling * solved), "layer", compose, identity, False
    )[2]
    lower_solved = solved + earlier_state
    return lower_solved.astype(jnp.bfloat16)[None]


def solution(mesh):
    placed = (
        P("layer", "dp", None),
        P("layer", "dp", None),
        P("layer", "dp", None),
        P("layer", None, None),
        P("layer", "dp"),
        P("layer", None),
    )
    return jax.shard_map(
        shards, mesh=mesh, in_specs=placed, out_specs=P("layer", "dp", None), check_vma=False
    )
```

profile of v0, /device:TPU:6, one launch (start us, length us, event | category | flops | bytes accessed | tf_op | source)
XLA Modules:
  0.0 1096.2 jit_solution(11241762447567834174)
XLA Ops:
  6.5 1.7 copy-done
  8.3 4.9 fusion.4
  13.3 419.7 %all-reduce.2.cloned.1.call-done = f32[2048,512]{1,0:T(8,128)} async-done(((f32[2048,512]{1,0:T(8,128)}), f32[2048,512]{1,0:T(8,128)}) %all-reduce.2.cloned.1.call-update) | async-done | bytes 4194320 | tf_op jit(solution)/shard_map/psum | solution.py:38
  433.0 1.7 constant_dynamic-slice_fusion.4
  434.7 108.1 %all-gather.3 = f32[32,1,512]{2,1,0:T(1,128)S(1)} all-gather(f32[1,1,512]{2,1,0:T(1,128)S(1)} %bitcast.60), channel_id=1, replica_groups=mesh['layer'=32,'dp'=16] {'layer'}, dimensions={0}, use_global_device_ids=true | all-gather | bytes 67584 | tf_op jit(solution)/shard_map/all_gather | solution.py:9
  542.8 102.3 %all-gather.2 = f32[32,1,128]{2,1,0:T(1,128)S(1)} all-gather(f32[1,1,128]{2,1,0:T(1,128)S(1)} %bitcast.64), channel_id=1, replica_groups=mesh['layer'=32,'dp'=16] {'layer'}, dimensions={0}, use_global_device_ids=true | all-gather | bytes 16896 | tf_op jit(solution)/shard_map/all_gather | solution.py:9
  645.1 32.3 %all-gather.10.cloned.1.call-done = f32[4096,512]{1,0:T(8,128)} async-done(((f32[128,512]{1,0:T(8,128)}), f32[4096,512]{1,0:T(8,128)}) %all-gather.10.cloned.1.call-update) | async-done | bytes 8388624 | tf_op jit(solution)/shard_map/all_gather | solution.py:9
  677.5 36.3 %while.30 = (s32[]{:T(128)}, f32[128,512]{1,0:T(8,128)S(1)}, s32[]{:T(128)}, f32[32,128,512]{2,1,0:T(8,128)}, f32[32,128]{1,0:T(8,128)S(1)}, /*index=5*/f32[32,5...) while((s32[]{:T(128)}, f32[128,512]{1,0:T(8,128)S(1)}, s32[]{:T(128)}, ...), condition=%wide.region_2.3_spmd.clone, body=%wide.region_1.2_spmd.clone.sunk | while | flops 327688 | bytes 794291 | solution.py:22
  677.5 1.1 fusion.21
  678.6 1.1 fusion.21
  679.8 1.1 fusion.21
  680.9 1.1 fusion.21
  682.1 1.1 fusion.21
  683.2 1.1 fusion.21
  684.3 1.1 fusion.21
  690.0 1.1 fusion.21
  691.2 1.1 fusion.21
  692.3 1.1 fusion.21
  693.4 1.1 fusion.21
  694.6 1.1 fusion.21
  701.4 1.1 fusion.21
  702.5 1.1 fusion.21
  703.7 1.1 fusion.21
  704.8 1.1 fusion.21
  705.9 1.1 fusion.21
  711.6 1.1 fusion.21
  712.8 1.1 fusion.21
  713.8 2.0 convolution_convert_fusion
  715.9 105.1 %all-gather.8.cloned.1.call-done = bf16[2048,512]{1,0:T(8,128)(2,1)} async-done(((bf16[128,512]{1,0:T(8,128)(2,1)}), bf16[2048,512]{1,0:T(8,128)(2,1)}) %all-gather.8.cloned.1.call-update) | async-done | bytes 2097168 | tf_op jit(solution)/shard_map/all_gather | solution.py:52
  821.0 2.9 multiply_multiply_fusion
  823.9 229.1 %all-gather.12.cloned.1.call-done = f32[4096,512]{1,0:T(8,128)} async-done(((f32[128,512]{1,0:T(8,128)}), f32[4096,512]{1,0:T(8,128)}) %all-gather.12.cloned.1.call-update) | async-done | bytes 8388624 | tf_op jit(solution)/shard_map/all_gather | solution.py:9
  1053.1 35.9 %while.31 = (s32[]{:T(128)}, f32[128,512]{1,0:T(8,128)S(1)}, s32[]{:T(128)}, f32[32,128,512]{2,1,0:T(8,128)}, f32[32,128]{1,0:T(8,128)S(1)}, /*index=5*/f32[32,512]{1,0:T(8,128)S(1)}, s32[]{:T(128)}, s32[]{:T(128)}) while((s32[]{:T(128)}, f32[128,512]{1,0:T(8,128)S(1)}, s32[]{:T(128)}, f32[32,128,512]{2,1,0:T(8,128)}, ...), condition=%wide.region_4.5_spmd.clone, body=%wide.region_3.4_spmd.clone.sunk | while | flops 327684 | bytes 794229 | solution.py:22
  (192 shorter events, 50.2 us)
Async XLA Ops:
  6.5 1.7 copy-start
  6.5 426.4 %all-reduce.2.cloned.1.call-start = ((), (), s32[]{:S(2)}) async-start(), calls=%async_computation | async-start | bytes 8388608 | tf_op jit(solution)/shard_map/psum | solution.py:38
  13.2 421.5 %copy-start.2 = (f32[1,512]{1,0:T(1,128)S(1)}, f32[1,512]{1,0:T(1,128)}, u32[]{:S(2)}) copy-start(f32[1,512]{1,0:T(1,128)} %param.15) | copy-start | bytes 6148
  13.2 529.6 %copy-start.3 = (f32[1,128]{1,0:T(1,128)S(1)}, f32[1,128]{1,0:T(1,128)}, u32[]{:S(2)}) copy-start(f32[1,128]{1,0:T(1,128)} %param.14) | copy-start | bytes 1540
  13.2 664.3 %all-gather.10.cloned.1.call-start = ((), (), s32[]{:S(2)}) async-start(), calls=%async_computation.2 | async-start | bytes 8650752 | tf_op jit(solution)/shard_map/all_gather | solution.py:9
  434.6 279.2 %copy-start.1 = (f32[128,512]{1,0:T(8,128)S(1)}, f32[128,512]{1,0:T(8,128)}, u32[]{:S(2)}) copy-start(f32[128,512]{1,0:T(8,128)} %constant_dynamic-slice_fusion.4) | copy-start | bytes 786436
  434.7 386.3 %all-gather.8.cloned.1.call-start = ((), (), s32[]{:S(2)}) async-start(), calls=%async_computation.1 | async-start | bytes 2228224 | tf_op jit(solution)/shard_map/all_gather | solution.py:52
  715.8 337.2 %all-gather.12.cloned.1.call-start = ((), (), s32[]{:S(2)}) async-start(), calls=%async_computation.3 | async-start | bytes 8650752 | tf_op jit(solution)/shard_map/all_gather | solution.py:9
Sparse Core Ops, SparseCore 0:
  13.3 419.5 all-reduce.1
  435.0 242.4 all-gather.9
  716.0 104.9 all-gather.7
  824.0 228.9 all-gather.11
where the time goes:
time: 1120 us; the launch traced here: 1100 us
  waiting for transfers between devices  786 us (70%)
  blocking collectives  210 us (19%)
  other arithmetic  68.8 us (6%)
  between operations  13.2 us (1%)
    psum x1, waiting for transfers between devices, shards(): summed = lax.psum(partial_full, 'dp')  420 us
    all_gather x2, waiting for transfers between devices, prefix(): everything = jax.tree.map(lambda part: lax.all_gather(part, axis), shard)  261 us
    all_gather x2, blocking collectives, prefix(): everything = jax.tree.map(lambda part: lax.all_gather(part, axis), shard)  210 us
    all_gather x1, waiting for transfers between devices, shards(): lax.all_gather(s_applied, 'dp', axis=0, tiled=True)  105 us
    select_n x64, other arithmetic, turn(): return jax.tree.map(lambda a, b: jnp.where(reached, a, b), new, before)  68.1 us
  transfers between devices with their start and end apart: 4, of which 4 were waited for; matrix products, arithmetic and copies ran while one was open for 0% of the time, Pallas kernels for 0%

commit v1 on v0

v1 whole, which is shorter than its diff:
```python
import jax
import jax.numpy as jnp
from jax import lax
from jax.experimental import pallas as pl
from jax.experimental.pallas import tpu as pltpu
from jax.sharding import PartitionSpec as P

MESH = pl.DeviceIdType.MESH
BF16 = jnp.bfloat16
F32 = jnp.float32

LAYERS, XS, ZL, YS, ZS = 32, 4, 8, 4, 16
TOK, DIN, DOUT, ROWS = 640, 2048, 512, 128


def off16(i):
    half = lax.div(i + 1, 2)
    return 8 + half * (1 - 2 * lax.rem(i, 2))


def off8(i):
    half = lax.div(i + 1, 2)
    return 4 + half * (1 - 2 * lax.rem(i, 2))


def kernel(
    acts, og, ainv, sinv, ind, outd, out,
    a_v, og_v, ai_v, si_v, ps, pr, v, so, sd, sf, ro, rd, rf, t, r, dk, dks, it, cpl, u, ul, sa, xs, rx, dd,
    ld_a, ld_o, ld_ai, ld_si, pair_s, pair_r, y_s, yo_r, yd_r, yf_r, dk_s, dk_r, r_s, r_r, u_s, u_r,
    sa_s, sa_r, sp_s, sp_r, x_s, x_r, d_s, d_r,
):
    lay = lax.axis_index("layer")
    dp = lax.axis_index("dp")
    x, zl = lax.div(lay, ZL), lax.rem(lay, ZL)
    y, zh, c = lax.div(dp, 4), lax.rem(lax.div(dp, 2), 2), lax.rem(dp, 2)
    z = zh * ZL + zl
    y1 = y + 1 - 2 * lax.rem(y, 2)
    y2 = lax.rem(y + 2, YS)
    y3 = YS - 1 - y
    oc = 1 - c
    me = zh * LAYERS + lay

    def at(layer, yy, hh, cc):
        return {"layer": layer, "dp": yy * 4 + hh * 2 + cc}

    partner = at(lay, y, zh, oc)
    near1 = at(lay, y1, zh, c)
    near3 = at(lay, y3, zh, c)

    barrier = pltpu.get_barrier_semaphore()

    def greet(i, carry):
        q = lax.rem(me + i, 2 * LAYERS)
        pl.semaphore_signal(
            barrier, inc=1, device_id=at(lax.rem(q, LAYERS), y, lax.div(q, LAYERS), c), device_id_type=MESH
        )
        return carry

    lax.fori_loop(1, 2 * LAYERS, greet, 0)
    for dev in (partner, near1, near3):
        pl.semaphore_signal(barrier, inc=1, device_id=dev, device_id_type=MESH)

    loads = []
    for jr in range(4):
        src = pl.multiple_of(lax.rem(x + jr, 4) * 128, 128)
        cp = pltpu.make_async_copy(og.at[0, :, pl.ds(src, 128)], og_v.at[:, pl.ds(jr * 128, 128)], ld_o)
        cp.start()
    for ci, cc in ((0, oc), (1, c)):
        for k, yy in enumerate((y2, y1, y3, y)):
            for h in range(2):
                src = pl.multiple_of(yy * 512 + h * 256 + cc * 128, 128)
                pltpu.make_async_copy(
                    acts.at[0, :, pl.ds(src, 128)], a_v.at[k, ci, :, pl.ds(h * 128, 128)], ld_a.at[k, ci]
                ).start()
    for ci, cc in ((0, oc), (1, c)):
        for k, yy in enumerate((y2, y1, y3, y)):
            for h in range(2):
                src = pl.multiple_of(yy * 512 + h * 256 + cc * 128, 128)
                pltpu.make_async_copy(
                    ainv.at[0, :, pl.ds(src, 128)], ai_v.at[k, ci, :, pl.ds(h * 128, 128)], ld_ai
                ).start()
    pltpu.make_async_copy(sinv.at[0], si_v, ld_si).start()

    dk[0:1, :] = ind[...]
    for j in range(4):
        dk[1 + j : 2 + j, :] = outd[0:1, j * 128 : (j + 1) * 128]

    pltpu.make_async_copy(og_v, og_v, ld_o).wait()

    def product(k, ci):
        pltpu.make_async_copy(a_v.at[k, ci], a_v.at[k, ci], ld_a.at[k, ci]).wait()
        return lax.dot_general(
            a_v[k, ci], og_v[...], (((0,), (0,)), ((), ())), preferred_element_type=F32
        )

    for k in range(4):
        g = product(k, 0)
        for j in range(4):
            ps[k, j] = g[:, j * 128 : (j + 1) * 128]
    for k in range(4):
        g = product(k, 1)
        for j in range(4):
            v[k, j] = g[:, j * 128 : (j + 1) * 128]

    pl.semaphore_wait(barrier, 2 * LAYERS - 1 + 3)

    def send(src, dst, ssem, rsem, dev):
        cp = pltpu.make_async_remote_copy(
            src_ref=src, dst_ref=dst, send_sem=ssem, recv_sem=rsem, device_id=dev, device_id_type=MESH
        )
        cp.start()

    def wait(ref, sem):
        pltpu.make_async_copy(ref, ref, sem).wait()

    for k in range(4):
        send(ps.at[k], pr.at[k], pair_s, pair_r.at[k], partner)

    def send_decay(i, carry):
        q = lax.rem(lay + i, LAYERS)
        send(dk, dks.at[lay], dk_s, dk_r, at(q, y, zh, c))
        return carry

    lax.fori_loop(1, LAYERS, send_decay, 0)
    pltpu.make_async_copy(dk, dks.at[lay], dk_r).start()

    first = (near1, near1, near3, near3)
    second = (near3, near3, near1, near1)
    k_first = (1, 1, 2, 2)
    k_second = (2, 2, 1, 1)
    wait(pr.at[0], pair_r.at[0])
    for j in (0, 2, 1, 3):
        so[j] = (v[0, j] + pr[0, j]).astype(BF16)
        send(so.at[j], ro.at[j], y_s, yo_r.at[j], first[j])
    wait(pr.at[1], pair_r.at[1])
    wait(pr.at[2], pair_r.at[2])
    for j in (0, 2, 1, 3):
        k = k_first[j]
        sd[j] = (v[k, j] + pr[k, j]).astype(BF16)
        send(sd.at[j], rd.at[j], y_s, yd_r.at[j], first[j])
    for j in (0, 2, 1, 3):
        k = k_second[j]
        wait(ro.at[j], yo_r.at[j])
        sf[j] = v[k, j] + pr[k, j] + ro[j].astype(F32)
        send(sf.at[j], rf.at[j], y_s, yf_r.at[j], second[j])
    wait(pr.at[3], pair_r.at[3])
    for j in (0, 2, 1, 3):
        wait(rd.at[j], yd_r.at[j])
        wait(rf.at[j], yf_r.at[j])
        total = v[3, j] + pr[3, j] + rd[j].astype(F32) + rf[j]
        t[j] = total.astype(BF16).reshape(ZS, 16, 128)
        xx = lax.rem(x + j, XS)

        def send_tile(i, carry, j=j, xx=xx):
            zz = lax.rem(z + off16(i), ZS)
            dev = at(xx * ZL + lax.rem(zz, ZL), y, lax.div(zz, ZL), c)
            send(t.at[j, zz], r.at[me], r_s, r_r, dev)
            return carry

        lax.fori_loop(0, 15 if j == 0 else 16, send_tile, 0)
        if j == 0:
            pltpu.make_async_copy(t.at[0, z], r.at[me], r_r).start()

    wait(dks, dk_r)
    rates = dks[:, 0, :]
    it[...] = jnp.concatenate([rates, jnp.zeros((128 - LAYERS, 128), F32)], axis=0).T
    mine = it[pl.ds(pl.multiple_of(zl * 16, 16), 16), :]
    for l in range(LAYERS):
        cpl[l] = mine[:, l : l + 1] * dks[l, pl.ds(1 + x, 1), :]

    wait(r, r_r)
    state = None
    for l in reversed(range(LAYERS)):
        grad = r[l].astype(F32) + r[LAYERS + l].astype(F32)
        state = grad if state is None else grad + cpl[l] * state
        u[l] = state.astype(BF16)

    spot = (pl.ds(pl.multiple_of(z * 16, 16), 16), pl.ds(pl.multiple_of(x * 128, 128), 128))
    for j in range(4):
        xx = lax.rem(x + j, XS)

        def send_upper(i, carry, j=j, xx=xx):
            zz = lax.rem(z + off16(i), ZS)
            ll = xx * ZL + lax.rem(zz, ZL)
            send(u.at[ll], ul.at[spot], u_s, u_r, at(ll, y, lax.div(zz, ZL), c))
            return carry

        lax.fori_loop(0, 15 if j == 0 else 16, send_upper, 0)
    pltpu.make_async_copy(u.at[lay], ul.at[spot], u_r).start()

    wait(si_v, ld_si)
    wait(ul, u_r)
    sa[3, 1] = jnp.dot(ul[...], si_v[...], preferred_element_type=F32).astype(BF16)

    half = (pl.ds(0, 128), pl.ds(128, 128))
    own = sa.at[3, 1]
    send(own.at[half[0]], sa.at[1, 1, half[0]], sa_s, sa_r.at[0], near1)
    send(own.at[half[1]], sa.at[2, 1, half[1]], sa_s, sa_r.at[1], near3)
    send(own.at[half[1]], sa.at[1, 1, half[1]], sa_s, sa_r.at[2], near1)
    send(own.at[half[0]], sa.at[2, 1, half[0]], sa_s, sa_r.at[3], near3)
    send(own, sa.at[3, 0], sp_s, sp_r.at[3], partner)

    wait(ai_v, ld_ai)
    acc = jnp.dot(ai_v[3, 1], sa[3, 1], preferred_element_type=F32)
    wait(sa.at[1, 1, half[0]], sa_r.at[0])
    send(sa.at[1, 1, half[0]], sa.at[0, 1, half[0]], sa_s, sa_r.at[4], near3)
    wait(sa.at[2, 1, half[1]], sa_r.at[1])
    send(sa.at[2, 1, half[1]], sa.at[0, 1, half[1]], sa_s, sa_r.at[5], near1)
    wait(sa.at[3, 0], sp_r.at[3])
    acc += jnp.dot(ai_v[3, 0], sa[3, 0], preferred_element_type=F32)
    wait(sa.at[1, 1, half[1]], sa_r.at[2])
    send(sa.at[1, 1], sa.at[1, 0], sp_s, sp_r.at[1], partner)
    wait(sa.at[2, 1, half[0]], sa_r.at[3])
    send(sa.at[2, 1], sa.at[2, 0], sp_s, sp_r.at[2], partner)
    acc += jnp.dot(ai_v[1, 1], sa[1, 1], preferred_element_type=F32)
    acc += jnp.dot(ai_v[2, 1], sa[2, 1], preferred_element_type=F32)
    wait(sa.at[1, 0], sp_r.at[1])
    acc += jnp.dot(ai_v[1, 0], sa[1, 0], preferred_element_type=F32)
    wait(sa.at[2, 0], sp_r.at[2])
    acc += jnp.dot(ai_v[2, 0], sa[2, 0], preferred_element_type=F32)
    wait(sa.at[0, 1, half[0]], sa_r.at[4])
    wait(sa.at[0, 1, half[1]], sa_r.at[5])
    send(sa.at[0, 1], sa.at[0, 0], sp_s, sp_r.at[0], partner)
    acc += jnp.dot(ai_v[0, 1], sa[0, 1], preferred_element_type=F32)
    wait(sa.at[0, 0], sp_r.at[0])
    acc += jnp.dot(ai_v[0, 0], sa[0, 0], preferred_element_type=F32)

    for j in range(4):
        xs[j] = acc[:, j * 128 : (j + 1) * 128].astype(BF16).reshape(ZL, 16, 128)
    for j in range(4):
        xx = lax.rem(x + j, XS)

        def send_solved(i, carry, xx=xx):
            zz = lax.rem(zl + off8(i), ZL)
            send(xs.at[xx, zz], rx.at[lay], x_s, x_r, at(xx * ZL + zz, y, zh, c))
            return carry

        lax.fori_loop(0, 7 if j == 0 else 8, send_solved, 0)
    pltpu.make_async_copy(xs.at[x, zl], rx.at[lay], x_r).start()

    wait(rx, x_r)
    state = None
    for l in range(LAYERS):
        solved = rx[l].astype(F32)
        state = solved if state is None else solved + cpl[l - 1] * state
        dd[l] = state.astype(BF16)

    place = (0, pl.ds(pl.multiple_of(zl * 16, 16), 16), pl.ds(pl.multiple_of(x * 128, 128), 128))
    for j in range(4):
        xx = lax.rem(x + j, XS)

        def send_lower(i, carry, xx=xx):
            zz = lax.rem(zl + off8(i), ZL)
            ll = xx * ZL + zz
            send(dd.at[ll], out.at[place], d_s, d_r, at(ll, y, zh, c))
            return carry

        lax.fori_loop(0, 7 if j == 0 else 8, send_lower, 0)
    pltpu.make_async_copy(dd.at[lay], out.at[place], d_r).start()

    wait(ps, pair_s)
    wait(so, y_s)
    wait(sd, y_s)
    wait(sf, y_s)
    wait(dks.at[pl.ds(0, LAYERS - 1)], dk_s)
    wait(r.at[pl.ds(0, 2 * LAYERS - 1)], r_s)
    wait(r.at[pl.ds(0, 2 * LAYERS - 1)], u_s)
    wait(sa.at[pl.ds(0, 1), 0], sa_s)
    wait(sa.at[pl.ds(0, 1), 0], sa_s)
    wait(sa.at[pl.ds(0, 1), 0], sa_s)
    wait(sa.at[:, 0], sp_s)
    wait(rx.at[pl.ds(0, LAYERS - 1)], x_s)
    wait(rx.at[pl.ds(0, LAYERS - 1)], d_s)
    wait(out, d_r)


def shards(activations, out_grads, a_inverse, s_inverse, in_decay, out_decay):
    vm = pltpu.VMEM
    dma = pltpu.SemaphoreType.DMA
    anywhere = pl.BlockSpec(memory_space=pl.ANY)
    inside = pl.BlockSpec(memory_space=pltpu.VMEM)
    unit = (4, 256, 128)
    scratch = [
        vm((4, 2, TOK, 256), BF16),
        vm((TOK, DOUT), BF16),
        vm((4, 2, ROWS, 256), BF16),
        vm((DOUT, DOUT), BF16),
        vm((4, 4, 256, 128), F32),
        vm((4, 4, 256, 128), F32),
        vm((4, 4, 256, 128), F32),
        vm(unit, BF16), vm(unit, BF16), vm(unit, F32),
        vm(unit, BF16), vm(unit, BF16), vm(unit, F32),
        vm((4, ZS, 16, 128), BF16),
        vm((2 * LAYERS, 16, 128), BF16),
        vm((8, 128), F32),
        vm((LAYERS, 8, 128), F32),
        vm((128, 128), F32),
        vm((LAYERS, 16, 128), F32),
        vm((LAYERS, 16, 128), BF16),
        vm((256, DOUT), BF16),
        vm((4, 2, 256, DOUT), BF16),
        vm((4, ZL, 16, 128), BF16),
        vm((LAYERS, 16, 128), BF16),
        vm((LAYERS, 16, 128), BF16),
        dma((4, 2)), dma(()), dma(()), dma(()),
        dma(()), dma((4,)),
        dma(()), dma((4,)), dma((4,)), dma((4,)),
        dma(()), dma(()),
        dma(()), dma(()),
        dma(()), dma(()),
        dma(()), dma((6,)),
        dma(()), dma((4,)),
        dma(()), dma(()),
        dma(()), dma(()),
    ]
    return pl.pallas_call(
        kernel,
        out_shape=jax.ShapeDtypeStruct((1, ROWS, DOUT), BF16),
        in_specs=[anywhere] * 4 + [inside] * 2,
        out_specs=inside,
        scratch_shapes=scratch,
        compiler_params=pltpu.CompilerParams(
            collective_id=0, has_side_effects=True, vmem_limit_bytes=48 * 1024 * 1024
        ),
    )(activations, out_grads, a_inverse, s_inverse, in_decay, out_decay)


def solution(mesh):
    placed = (
        P("layer", "dp", None),
        P("layer", "dp", None),
        P("layer", "dp", None),
        P("layer", None, None),
        P("layer", "dp"),
        P("layer", None),
    )
    return jax.shard_map(
        shards, mesh=mesh, in_specs=placed, out_specs=P("layer", "dp", None), check_vma=False
    )
```

time: 1120 us -> 101 us (0.09); the launches traced: 1100 us -> 101 us
  waiting for transfers between devices: 786 us -> 0 us
  blocking collectives: 210 us -> 0 us
  Pallas kernels: 0 us -> 93.8 us
  other arithmetic: 68.8 us -> 0 us
  between operations: 13.2 us -> 0.02 us
    psum x1 -> x0, waiting for transfers between devices: 420 us -> none  [shards(): summed = lax.psum(partial_full, 'dp')]
    all_gather x3 -> x0, waiting for transfers between devices: 367 us -> none  [the longest x2 261 us: prefix(): everything = jax.tree.map(lambda part: lax.all_gather(part, axis), shard)]
    all_gather x2 -> x0, blocking collectives: 210 us -> none  [prefix(): everything = jax.tree.map(lambda part: lax.all_gather(part, axis), shard)]
    pallas_call x0 -> x1, Pallas kernels: none -> 93.8 us  [shards(): pl.pallas_call(kernel, out_shape=jax.ShapeDtypeStruct((1, ROWS, DOUT), BF...]
    select_n x64 -> x0, other arithmetic: 68.1 us -> none  [turn(): return jax.tree.map(lambda a, b: jnp.where(reached, a, b), new, before)]
  transfers between devices with their start and end apart: 4 -> 0, of which waited for: 4 -> 0; matrix products, arithmetic and copies ran while one was open for 0% -> 0% of each run, Pallas kernels for 0% -> 0%
where the time goes in v1:
time: 101 us
  Pallas kernels  93.8 us (93%)
  local copies, waits for them, and re-layouts  6.9 us (7%)
    pallas_call x1, Pallas kernels, shards(): pl.pallas_call(kernel, out_shape=jax.ShapeDtypeStruct((1, ROWS, DOUT), BF...  93.8 us
    unnamed x13, local copies, waits for them, and re-layouts  6.9 us

profile of v1, /device:TPU:6, one launch (start us, length us, event | category | flops | bytes accessed | tf_op | source)
XLA Modules:
  0.0 100.8 jit_solution(10659216298593782581)
XLA Ops:
  0.0 0.0 copy-start
  0.0 1.7 %copy-done = bf16[1,640,2048]{2,1,0:T(8,128)(2,1)S(1)} copy-done((bf16[1,640,2048]{2,1,0:T(8,128)(2,1)S(1)}, bf16[1,640,2048]{2,1,0:T(8,128)(2,1)}, u32[]{:S(2)}) %copy-start) | copy-done | bytes 2621464
  1.7 0.0 copy-start.1
  1.7 1.1 %copy-done.1 = bf16[1,640,512]{2,1,0:T(8,128)(2,1)S(1)} copy-done((bf16[1,640,512]{2,1,0:T(8,128)(2,1)S(1)}, bf16[1,640,512]{2,1,0:T(8,128)(2,1)}, u32[]{:S(2)}) %copy-start.1) | copy-done | bytes 655384
  2.8 0.0 copy-start.2
  2.8 1.0 %copy-done.2 = bf16[1,128,2048]{2,1,0:T(8,128)(2,1)S(1)} copy-done((bf16[1,128,2048]{2,1,0:T(8,128)(2,1)S(1)}, bf16[1,128,2048]{2,1,0:T(8,128)(2,1)}, u32[]{:S(2)}) %copy-start.2) | copy-done | bytes 524312
  3.9 0.0 copy-start.3
  3.9 1.0 %copy-done.3 = bf16[1,512,512]{2,1,0:T(8,128)(2,1)S(1)} copy-done((bf16[1,512,512]{2,1,0:T(8,128)(2,1)S(1)}, bf16[1,512,512]{2,1,0:T(8,128)(2,1)}, u32[]{:S(2)}) %copy-start.3) | copy-done | bytes 524312
  4.9 0.0 copy-start.4
  4.9 0.7 copy-done.4
  5.6 0.0 copy-start.5
  5.6 0.7 copy-done.5
  6.3 93.8 %shard_map.64 = bf16[1,128,512]{2,1,0:T(8,128)(2,1)S(1)} custom-call(bf16[1,640,2048]{2,1,0:T(8,128)(2,1)S(1)} %copy-done, bf16[1,640,512]{2,1,0:T(8,128)(2,1)S(1)} %copy-done.1, bf16[1,128,2048]{2,1,0:T(8,128)(2,1)S(1)} %copy-done.2, bf16[1,512,512]{2,1,0:T(8,128)(2,1)S(1)} %copy-done.3, f32[1,128]{1,0:T(1,128)S(1)} %copy-done.5, f32[1,512]{1,0:T(1,128)S(1)} %copy-done.4), custom_call_target="tpu_custom_call" | custom-call | tf_op jit(solution)/shard_map/pallas_call | solution.py:316
  100.1 0.7 copy.8
Async XLA Ops:
  0.0 1.7 %copy-start = (bf16[1,640,2048]{2,1,0:T(8,128)(2,1)S(1)}, bf16[1,640,2048]{2,1,0:T(8,128)(2,1)}, u32[]{:S(2)}) copy-start(bf16[1,640,2048]{2,1,0:T(8,128)(2,1)} %acts.1) | copy-start | bytes 7864324
  1.7 1.1 %copy-start.1 = (bf16[1,640,512]{2,1,0:T(8,128)(2,1)S(1)}, bf16[1,640,512]{2,1,0:T(8,128)(2,1)}, u32[]{:S(2)}) copy-start(bf16[1,640,512]{2,1,0:T(8,128)(2,1)} %og.1) | copy-start | bytes 1966084
  2.8 1.0 %copy-start.2 = (bf16[1,128,2048]{2,1,0:T(8,128)(2,1)S(1)}, bf16[1,128,2048]{2,1,0:T(8,128)(2,1)}, u32[]{:S(2)}) copy-start(bf16[1,128,2048]{2,1,0:T(8,128)(2,1)} %ainv.1) | copy-start | bytes 1572868
  3.9 1.0 %copy-start.3 = (bf16[1,512,512]{2,1,0:T(8,128)(2,1)S(1)}, bf16[1,512,512]{2,1,0:T(8,128)(2,1)}, u32[]{:S(2)}) copy-start(bf16[1,512,512]{2,1,0:T(8,128)(2,1)} %sinv.1) | copy-start | bytes 1572868
  4.9 0.7 copy-start.4
  5.6 0.7 copy-start.5

commit v2 on v1

--- a/solution.py
+++ b/solution.py
@@ -25,8 +25,8 @@
 
 def kernel(
     acts, og, ainv, sinv, ind, outd, out,
-    a_v, og_v, ai_v, si_v, ps, pr, v, so, sd, sf, ro, rd, rf, t, r, dk, dks, it, cpl, u, ul, sa, xs, rx, dd,
-    ld_a, ld_o, ld_ai, ld_si, pair_s, pair_r, y_s, yo_r, yd_r, yf_r, dk_s, dk_r, r_s, r_r, u_s, u_r,
+    a_v, og_v, og_t, ai_v, si_v, ind_v, outd_v, g, pr, so, sd, sf, ro, rd, rf, t, r, dk, dks, it, cpl, u, ul, sa, xs, rx, dd,
+    ld_a, ld_o, ld_ai, ld_si, ld_d, round_s, pair_s, pair_r, y_s, yo_r, yd_r, yf_r, dk_s, dk_r, r_s, r_r, u_s, u_r,
     sa_s, sa_r, sp_s, sp_r, x_s, x_r, d_s, d_r,
 ):
     lay = lax.axis_index("layer")
@@ -47,31 +47,36 @@
     near1 = at(lay, y1, zh, c)
     near3 = at(lay, y3, zh, c)
 
+    def send(src, dst, ssem, rsem, dev):
+        pltpu.make_async_remote_copy(
+            src_ref=src, dst_ref=dst, send_sem=ssem, recv_sem=rsem, device_id=dev, device_id_type=MESH
+        ).start()
+
+    def wait(ref, sem):
+        pltpu.make_async_copy(ref, ref, sem).wait()
+
+    def signal(sem, dev):
+        pl.semaphore_signal(sem, inc=1, device_id=dev, device_id_type=MESH)
+
+    def along_z(step):
+        zz = lax.rem(z + step + ZS, ZS)
+        return at(x * ZL + lax.rem(zz, ZL), y, lax.div(zz, ZL), c)
+
+    def along_x(step):
+        return at(lax.rem(x + step, XS) * ZL + zl, y, zh, c)
+
     barrier = pltpu.get_barrier_semaphore()
-
-    def greet(i, carry):
-        q = lax.rem(me + i, 2 * LAYERS)
-        pl.semaphore_signal(
-            barrier, inc=1, device_id=at(lax.rem(q, LAYERS), y, lax.div(q, LAYERS), c), device_id_type=MESH
-        )
-        return carry
-
-    lax.fori_loop(1, 2 * LAYERS, greet, 0)
-    for dev in (partner, near1, near3):
-        pl.semaphore_signal(barrier, inc=1, device_id=dev, device_id_type=MESH)
-
-    loads = []
+    for dev in (partner, near1, near3, along_z(1), along_z(-1), along_x(1), along_x(2), along_x(3)):
+        signal(barrier, dev)
+
     for jr in range(4):
         src = pl.multiple_of(lax.rem(x + jr, 4) * 128, 128)
-        cp = pltpu.make_async_copy(og.at[0, :, pl.ds(src, 128)], og_v.at[:, pl.ds(jr * 128, 128)], ld_o)
-        cp.start()
-    for ci, cc in ((0, oc), (1, c)):
-        for k, yy in enumerate((y2, y1, y3, y)):
-            for h in range(2):
-                src = pl.multiple_of(yy * 512 + h * 256 + cc * 128, 128)
-                pltpu.make_async_copy(
-                    acts.at[0, :, pl.ds(src, 128)], a_v.at[k, ci, :, pl.ds(h * 128, 128)], ld_a.at[k, ci]
-                ).start()
+        pltpu.make_async_copy(og.at[0, :, pl.ds(src, 128)], og_v.at[:, pl.ds(jr * 128, 128)], ld_o).start()
+    for i in range(5):
+        rows = pl.ds(i * 128, 128)
+        pltpu.make_async_copy(acts.at[0, rows], a_v.at[rows], ld_a).start()
+    pltpu.make_async_copy(ind, ind_v, ld_d.at[0]).start()
+    pltpu.make_async_copy(outd, outd_v, ld_d.at[1]).start()
     for ci, cc in ((0, oc), (1, c)):
         for k, yy in enumerate((y2, y1, y3, y)):
             for h in range(2):
@@ -81,48 +86,39 @@
                 ).start()
     pltpu.make_async_copy(sinv.at[0], si_v, ld_si).start()
 
-    dk[0:1, :] = ind[...]
-    for j in range(4):
-        dk[1 + j : 2 + j, :] = outd[0:1, j * 128 : (j + 1) * 128]
-
-    pltpu.make_async_copy(og_v, og_v, ld_o).wait()
-
-    def product(k, ci):
-        pltpu.make_async_copy(a_v.at[k, ci], a_v.at[k, ci], ld_a.at[k, ci]).wait()
-        return lax.dot_general(
-            a_v[k, ci], og_v[...], (((0,), (0,)), ((), ())), preferred_element_type=F32
-        )
-
-    for k in range(4):
-        g = product(k, 0)
-        for j in range(4):
-            ps[k, j] = g[:, j * 128 : (j + 1) * 128]
-    for k in range(4):
-        g = product(k, 1)
-        for j in range(4):
-            v[k, j] = g[:, j * 128 : (j + 1) * 128]
-
-    pl.semaphore_wait(barrier, 2 * LAYERS - 1 + 3)
-
-    def send(src, dst, ssem, rsem, dev):
-        cp = pltpu.make_async_remote_copy(
-            src_ref=src, dst_ref=dst, send_sem=ssem, recv_sem=rsem, device_id=dev, device_id_type=MESH
-        )
-        cp.start()
-
-    def wait(ref, sem):
-        pltpu.make_async_copy(ref, ref, sem).wait()
-
-    for k in range(4):
-        send(ps.at[k], pr.at[k], pair_s, pair_r.at[k], partner)
-
-    def send_decay(i, carry):
-        q = lax.rem(lay + i, LAYERS)
-        send(dk, dks.at[lay], dk_s, dk_r, at(q, y, zh, c))
-        return carry
-
-    lax.fori_loop(1, LAYERS, send_decay, 0)
-    pltpu.make_async_copy(dk, dks.at[lay], dk_r).start()
+    wait(og_v, ld_o)
+    og_t[...] = og_v[...].T
+    wait(a_v, ld_a)
+
+    def product(k, yy):
+        for h in range(2):
+            src = pl.multiple_of(yy * 512 + h * 256, 256)
+            part = jnp.dot(og_t[...], a_v[:, pl.ds(src, 256)], preferred_element_type=F32)
+            for cc in range(2):
+                for j in range(4):
+                    g[cc, k, j, h] = part[j * 128 : (j + 1) * 128, cc * 128 : (cc + 1) * 128]
+
+    product(0, y2)
+    pl.semaphore_wait(barrier, 8)
+    send(g.at[oc, 0], pr.at[0], pair_s, pair_r.at[0], partner)
+    signal(round_s.at[0], along_z(1))
+    signal(round_s.at[0], along_z(-1))
+    product(1, y1)
+    send(g.at[oc, 1], pr.at[1], pair_s, pair_r.at[1], partner)
+    product(2, y3)
+    send(g.at[oc, 2], pr.at[2], pair_s, pair_r.at[2], partner)
+    pl.semaphore_wait(round_s.at[0], 2)
+    signal(round_s.at[1], along_z(2))
+    signal(round_s.at[1], along_z(-2))
+    product(3, y)
+    send(g.at[oc, 3], pr.at[3], pair_s, pair_r.at[3], partner)
+
+    wait(ind_v, ld_d.at[0])
+    wait(outd_v, ld_d.at[1])
+    dk[...] = jnp.zeros_like(dk)
+    dk[0:1, :] = ind_v[...]
+    for j in range(4):
+        dk[1 + j : 2 + j, :] = outd_v[0:1, j * 128 : (j + 1) * 128]
 
     first = (near1, near1, near3, near3)
     second = (near3, near3, near1, near1)
@@ -130,25 +126,43 @@
     k_second = (2, 2, 1, 1)
     wait(pr.at[0], pair_r.at[0])
     for j in (0, 2, 1, 3):
-        so[j] = (v[0, j] + pr[0, j]).astype(BF16)
+        so[j] = (g[c, 0, j] + pr[0, j]).astype(BF16)
         send(so.at[j], ro.at[j], y_s, yo_r.at[j], first[j])
+    pl.semaphore_wait(round_s.at[1], 2)
+    signal(round_s.at[2], along_z(4))
+    signal(round_s.at[2], along_z(-4))
     wait(pr.at[1], pair_r.at[1])
     wait(pr.at[2], pair_r.at[2])
     for j in (0, 2, 1, 3):
         k = k_first[j]
-        sd[j] = (v[k, j] + pr[k, j]).astype(BF16)
+        sd[j] = (g[c, k, j] + pr[k, j]).astype(BF16)
         send(sd.at[j], rd.at[j], y_s, yd_r.at[j], first[j])
+    pl.semaphore_wait(round_s.at[2], 2)
+    for step in range(1, XS):
+        signal(round_s.at[3], along_x(step))
     for j in (0, 2, 1, 3):
         k = k_second[j]
         wait(ro.at[j], yo_r.at[j])
-        sf[j] = v[k, j] + pr[k, j] + ro[j].astype(F32)
+        sf[j] = g[c, k, j] + pr[k, j] + ro[j].astype(F32)
         send(sf.at[j], rf.at[j], y_s, yf_r.at[j], second[j])
+
+    pl.semaphore_wait(round_s.at[3], XS - 1)
+
+    def send_decay(i, carry):
+        q = lax.rem(lay + i, LAYERS)
+        send(dk, dks.at[lay], dk_s, dk_r, at(q, y, zh, c))
+        return carry
+
+    lax.fori_loop(1, LAYERS, send_decay, 0)
+    pltpu.make_async_copy(dk, dks.at[lay], dk_r).start()
+
     wait(pr.at[3], pair_r.at[3])
     for j in (0, 2, 1, 3):
         wait(rd.at[j], yd_r.at[j])
         wait(rf.at[j], yf_r.at[j])
-        total = v[3, j] + pr[3, j] + rd[j].astype(F32) + rf[j]
-        t[j] = total.astype(BF16).reshape(ZS, 16, 128)
+        total = g[c, 3, j] + pr[3, j] + rd[j].astype(F32) + rf[j]
+        for h in range(2):
+            t[j, h * ZL : (h + 1) * ZL] = total[h].T.astype(BF16).reshape(ZL, 16, 128)
         xx = lax.rem(x + j, XS)
 
         def send_tile(i, carry, j=j, xx=xx):
@@ -258,7 +272,7 @@
         lax.fori_loop(0, 7 if j == 0 else 8, send_lower, 0)
     pltpu.make_async_copy(dd.at[lay], out.at[place], d_r).start()
 
-    wait(ps, pair_s)
+    wait(pr, pair_s)
     wait(so, y_s)
     wait(sd, y_s)
     wait(sf, y_s)
@@ -277,17 +291,19 @@
 def shards(activations, out_grads, a_inverse, s_inverse, in_decay, out_decay):
     vm = pltpu.VMEM
     dma = pltpu.SemaphoreType.DMA
-    anywhere = pl.BlockSpec(memory_space=pl.ANY)
+    outside = pl.BlockSpec(memory_space=pltpu.HBM)
     inside = pl.BlockSpec(memory_space=pltpu.VMEM)
-    unit = (4, 256, 128)
+    unit = (4, 2, 128, 128)
     scratch = [
-        vm((4, 2, TOK, 256), BF16),
+        vm((TOK, DIN), BF16),
         vm((TOK, DOUT), BF16),
+        vm((DOUT, TOK), BF16),
         vm((4, 2, ROWS, 256), BF16),
         vm((DOUT, DOUT), BF16),
-        vm((4, 4, 256, 128), F32),
-        vm((4, 4, 256, 128), F32),
-        vm((4, 4, 256, 128), F32),
+        vm((1, ROWS), F32),
+        vm((1, DOUT), F32),
+        vm((2, 4, 4, 2, 128, 128), F32),
+        vm((4, 4, 2, 128, 128), F32),
         vm(unit, BF16), vm(unit, BF16), vm(unit, F32),
         vm(unit, BF16), vm(unit, BF16), vm(unit, F32),
         vm((4, ZS, 16, 128), BF16),
@@ -302,7 +318,8 @@
         vm((4, ZL, 16, 128), BF16),
         vm((LAYERS, 16, 128), BF16),
         vm((LAYERS, 16, 128), BF16),
-        dma((4, 2)), dma(()), dma(()), dma(()),
+        dma(()), dma(()), dma(()), dma(()), dma((2,)),
+        pltpu.SemaphoreType.REGULAR((4,)),
         dma(()), dma((4,)),
         dma(()), dma((4,)), dma((4,)), dma((4,)),
         dma(()), dma(()),
@@ -316,11 +333,11 @@
     return pl.pallas_call(
         kernel,
         out_shape=jax.ShapeDtypeStruct((1, ROWS, DOUT), BF16),
-        in_specs=[anywhere] * 4 + [inside] * 2,
+        in_specs=[outside] * 6,
         out_specs=inside,
         scratch_shapes=scratch,
         compiler_params=pltpu.CompilerParams(
-            collective_id=0, has_side_effects=True, vmem_limit_bytes=48 * 1024 * 1024
+            collective_id=0, has_side_effects=True, vmem_limit_bytes=67043328
         ),
     )(activations, out_grads, a_inverse, s_inverse, in_decay, out_decay)
 

time: 101 us -> 92.3 us (0.914)
  local copies, waits for them, and re-layouts: 6.9 us -> 1.57 us
  Pallas kernels: 93.8 us -> 90.6 us
    unnamed x13 -> x1, local copies, waits for them, and re-layouts: 6.9 us -> 1.57 us
    pallas_call x1, Pallas kernels: 93.8 us -> 90.6 us  [shards(): pl.pallas_call(kernel, out_shape=jax.ShapeDtypeStruct((1, ROWS, DOUT), BF...]
where the time goes in v2:
time: 92.3 us; the launch traced here: 92.2 us
  Pallas kernels  90.6 us (98%)
  local copies, waits for them, and re-layouts  1.57 us (2%)
    pallas_call x1, Pallas kernels, shards(): pl.pallas_call(kernel, out_shape=jax.ShapeDtypeStruct((1, ROWS, DOUT), BF...  90.6 us

profile of v2, /device:TPU:6, one launch (start us, length us, event | category | flops | bytes accessed | tf_op | source)
XLA Modules:
  0.0 92.2 jit_solution(12580303915815364678)
XLA Ops:
  0.0 90.6 %shard_map.64 = bf16[1,128,512]{2,1,0:T(8,128)(2,1)} custom-call(bf16[1,640,2048]{2,1,0:T(8,128)(2,1)} %acts.1, bf16[1,640,512]{2,1,0:T(8,128)(2,1)} %og.1, bf16[1,128,2048]{2,1,0:T(8,128)(2,1)} %ainv.1, bf16[1,512,512]{2,1,0:T(8,128)(2,1)} %sinv.1, f32[1,128]{1,0:T(1,128)} %ind.1, f32[1,512]{1,0:T(1,128)} %outd.1), custom_call_target="tpu_custom_call" | custom-call | tf_op jit(solution)/shard_map/pallas_call | solution.py:333
  90.6 1.6 %copy.8 = bf16[1,128,512]{2,1,0:T(8,128)(2,1)} copy(bf16[1,128,512]{2,1,0:T(8,128)(2,1)} %shard_map.64) | data formatting | bytes 262144

commit v3 on v2

v3 whole, which is shorter than its diff:
```python
import jax
import jax.numpy as jnp
from jax import lax
from jax.experimental import pallas as pl
from jax.experimental.pallas import tpu as pltpu
from jax.sharding import PartitionSpec as P

MESH = pl.DeviceIdType.MESH
BF16 = jnp.bfloat16
F32 = jnp.float32

LAYERS, XS, ZL, YS, ZS = 32, 4, 8, 4, 16
TOK, DIN, DOUT, ROWS = 640, 2048, 512, 128


def off8(i):
    half = lax.div(i + 1, 2)
    return 4 + half * (1 - 2 * lax.rem(i, 2))


def kernel(
    acts, og, ainv, sinv, ind, outd, out,
    a_v, og_v, og_t, ai_v, si_v, ind_v, outd_v, g, pr, so, sd, sf, ro, rd, rf, t, r, dk, dks, it, cpl, u, ul, sa, xs, rx, dd, ot,
    ld_a, ld_o, ld_ai, ld_si, ld_d, round_s, pair_s, pair_r, y_s, yo_r, yd_r, yf_r, dk_s, dk_r, r_s, r_r, u_s, u_r,
    sa_s, sa_r, sp_s, sp_r, x_s, x_r, d_s, d_r,
):
    lay = lax.axis_index("layer")
    dp = lax.axis_index("dp")
    x, zl = lax.div(lay, ZL), lax.rem(lay, ZL)
    y, zh, c = lax.div(dp, 4), lax.rem(lax.div(dp, 2), 2), lax.rem(dp, 2)
    z = zh * ZL + zl
    y1 = y + 1 - 2 * lax.rem(y, 2)
    y2 = lax.rem(y + 2, YS)
    y3 = YS - 1 - y
    oc = 1 - c
    me = zh * LAYERS + lay

    def at(layer, yy, hh, cc):
        return {"layer": layer, "dp": yy * 4 + hh * 2 + cc}

    partner = at(lay, y, zh, oc)
    near1 = at(lay, y1, zh, c)
    near2 = at(lay, y2, zh, c)
    near3 = at(lay, y3, zh, c)

    def send(src, dst, ssem, rsem, dev):
        pltpu.make_async_remote_copy(
            src_ref=src, dst_ref=dst, send_sem=ssem, recv_sem=rsem, device_id=dev, device_id_type=MESH
        ).start()

    def wait(ref, sem):
        pltpu.make_async_copy(ref, ref, sem).wait()

    def signal(sem, dev):
        pl.semaphore_signal(sem, inc=1, device_id=dev, device_id_type=MESH)

    def along_z(step):
        zz = lax.rem(z + step + ZS, ZS)
        return at(x * ZL + lax.rem(zz, ZL), y, lax.div(zz, ZL), c)

    def along_x(step):
        return at(lax.rem(x + step, XS) * ZL + zl, y, zh, c)

    barrier = pltpu.get_barrier_semaphore()
    for dev in (partner, near1, near2, near3, along_z(1), along_z(-1), along_x(1), along_x(2), along_x(3)):
        signal(barrier, dev)

    for jr in range(4):
        src = pl.multiple_of(lax.rem(x + jr, 4) * 128, 128)
        pltpu.make_async_copy(og.at[0, :, pl.ds(src, 128)], og_v.at[:, pl.ds(jr * 128, 128)], ld_o).start()
    for i in range(5):
        rows = pl.ds(i * 128, 128)
        pltpu.make_async_copy(acts.at[0, rows], a_v.at[rows], ld_a).start()
    pltpu.make_async_copy(ind, ind_v, ld_d.at[0]).start()
    pltpu.make_async_copy(outd, outd_v, ld_d.at[1]).start()
    for ci, cc in ((0, oc), (1, c)):
        for k, yy in enumerate((y2, y1, y3, y)):
            for h in range(2):
                src = pl.multiple_of(yy * 512 + h * 256 + cc * 128, 128)
                pltpu.make_async_copy(
                    ainv.at[0, :, pl.ds(src, 128)], ai_v.at[k, ci, :, pl.ds(h * 128, 128)], ld_ai
                ).start()
    pltpu.make_async_copy(sinv.at[0], si_v, ld_si).start()

    wait(og_v, ld_o)
    og_t[...] = og_v[...].T
    wait(a_v, ld_a)

    def product(k, yy):
        for h in range(2):
            src = pl.multiple_of(yy * 512 + h * 256, 256)
            part = jnp.dot(og_t[...], a_v[:, pl.ds(src, 256)], preferred_element_type=F32)
            for cc in range(2):
                for j in range(4):
                    g[cc, k, j, h] = part[j * 128 : (j + 1) * 128, cc * 128 : (cc + 1) * 128]

    product(0, y2)
    pl.semaphore_wait(barrier, 9)
    send(g.at[oc, 0], pr.at[0], pair_s, pair_r.at[0], partner)
    signal(round_s.at[0], along_z(1))
    signal(round_s.at[0], along_z(-1))
    product(1, y1)
    send(g.at[oc, 1], pr.at[1], pair_s, pair_r.at[1], partner)
    product(2, y3)
    send(g.at[oc, 2], pr.at[2], pair_s, pair_r.at[2], partner)
    pl.semaphore_wait(round_s.at[0], 2)
    signal(round_s.at[1], along_z(2))
    signal(round_s.at[1], along_z(-2))
    product(3, y)
    send(g.at[oc, 3], pr.at[3], pair_s, pair_r.at[3], partner)

    wait(ind_v, ld_d.at[0])
    wait(outd_v, ld_d.at[1])
    for j in range(XS):
        dk[j, 0:1, :] = ind_v[...]
        dk[j, 1:2, :] = outd_v[0:1, j * 128 : (j + 1) * 128]

    first = (near1, near1, near3, near3)
    second = (near3, near3, near1, near1)
    k_first = (1, 1, 2, 2)
    k_second = (2, 2, 1, 1)
    halves = (1 - zh, zh)
    chunks = (((0, 0), (2, 0)), ((0, 1), (2, 1)), ((1, 0), (3, 0)), ((1, 1), (3, 1)))

    def pair_sum(k, j, h):
        return g[c, k, j, halves[h]] + pr[k, j, halves[h]]

    def send_far(n):
        for j, h in chunks[n]:
            so[j, h] = pair_sum(0, j, h).astype(BF16)
            send(so.at[j, h], ro.at[j, h], y_s, yo_r.at[j, h], first[j])

    def send_first(n):
        for j, h in chunks[n]:
            sd[j, h] = pair_sum(k_first[j], j, h).astype(BF16)
            send(sd.at[j, h], rd.at[j, h], y_s, yd_r.at[j, h], first[j])

    def send_second(n):
        for j, h in chunks[n]:
            wait(ro.at[j, h], yo_r.at[j, h])
            sf[j, h] = pair_sum(k_second[j], j, h) + ro[j, h].astype(F32)
            send(sf.at[j, h], rf.at[j, h], y_s, yf_r.at[j, h], second[j])

    def send_tiles(n):
        for j, h in chunks[n]:
            wait(rd.at[j, h], yd_r.at[j, h])
            wait(rf.at[j, h], yf_r.at[j, h])
            total = pair_sum(3, j, h) + rd[j, h].astype(F32) + rf[j, h]
            t[j, h] = total.T.astype(BF16).reshape(ZL, 16, 128)
            xx = lax.rem(x + j, XS)

            def send_tile(i, carry, j=j, h=h, xx=xx):
                zz = lax.rem(zl + off8(i), ZL)
                send(t.at[j, h, zz], r.at[me], r_s, r_r, at(xx * ZL + zz, y, halves[h], c))
                return carry

            here = j == 0 and h == 1
            lax.fori_loop(0, 7 if here else 8, send_tile, 0)
            if here:
                pltpu.make_async_copy(t.at[0, 1, zl], r.at[me], r_r).start()

    def send_decay(i, carry):
        q = lax.rem(lay + i, LAYERS)
        send(dk.at[lax.div(q, ZL)], dks.at[lay], dk_s, dk_r, at(q, y, zh, c))
        return carry

    wait(pr.at[0], pair_r.at[0])
    send_far(0)
    wait(pr.at[1], pair_r.at[1])
    wait(pr.at[2], pair_r.at[2])
    send_first(0)
    send_far(1)
    pl.semaphore_wait(round_s.at[1], 2)
    signal(round_s.at[2], along_z(4))
    signal(round_s.at[2], along_z(-4))
    send_second(0)
    send_first(1)
    send_far(2)
    pl.semaphore_wait(round_s.at[2], 2)
    for step in range(1, XS):
        signal(round_s.at[3], along_x(step))
    send_second(1)
    send_first(2)
    send_far(3)
    pl.semaphore_wait(round_s.at[3], XS - 1)
    lax.fori_loop(1, LAYERS, send_decay, 0)
    pltpu.make_async_copy(dk.at[x], dks.at[lay], dk_r).start()
    wait(pr.at[3], pair_r.at[3])
    send_tiles(0)
    send_second(2)
    send_first(3)
    send_tiles(1)
    send_second(3)
    send_tiles(2)
    send_tiles(3)

    wait(dks, dk_r)
    rates = dks[:, 0, :]
    it[...] = jnp.concatenate([rates, jnp.zeros((128 - LAYERS, 128), F32)], axis=0).T
    mine = it[pl.ds(pl.multiple_of(zl * 16, 16), 16), :]
    for l in range(LAYERS):
        cpl[l] = mine[:, l : l + 1] * dks[l, 1:2, :]

    wait(r, r_r)
    state = None
    for l in reversed(range(LAYERS)):
        grad = r[l].astype(F32) + r[LAYERS + l].astype(F32)
        state = grad if state is None else grad + cpl[l] * state
        u[l] = state.astype(BF16)

    block = lax.div(z, 4)
    order = (0, 1, 3, 2)
    for d in order:

        def send_upper(i, carry, d=d):
            xx = lax.rem(x + lax.div(i + 1, 4), XS)
            zz = lax.rem(block + d, 4) * 4 + lax.rem(z + i + 1, 4)
            ll = xx * ZL + lax.rem(zz, ZL)
            send(u.at[ll], ul.at[z, x], u_s.at[d], u_r.at[(4 - d) % 4], at(ll, y, lax.div(zz, ZL), c))
            return carry

        lax.fori_loop(0, 15 if d == 0 else 16, send_upper, 0)
        if d == 0:
            pltpu.make_async_copy(u.at[lay], ul.at[z, x], u_r.at[0]).start()

    def rows_of(d, start=0, size=64):
        return pl.ds(pl.multiple_of(lax.rem(block + d, 4) * 64 + start, size), size)

    wait(si_v, ld_si)

    def side_s(d):
        rows = rows_of(d)
        places = pl.ds(lax.rem(block + d, 4) * 4, 4)
        wait(ul.at[places], u_r.at[d])
        upper = jnp.concatenate([ul[places, j].reshape(64, 128) for j in range(XS)], axis=1)
        sa[3, 1, rows] = jnp.dot(upper, si_v[...], preferred_element_type=F32).astype(BF16)
        src = sa.at[3, 1, rows]
        send(src, sa.at[1, 1, rows], sa_s, sa_r.at[0, d], near1)
        send(src, sa.at[2, 1, rows], sa_s, sa_r.at[1, d], near3)
        if d == order[3]:
            send(src, sa.at[0, 1, rows], sa_s, sa_r.at[2, d], near2)
        send(src, sa.at[3, 0, rows], sp_s, sp_r.at[3, d], partner)

    def pass_on(d):
        rows = rows_of(d)
        low, high = rows_of(d, 0, 32), rows_of(d, 32, 32)
        wait(sa.at[1, 1, rows], sa_r.at[0, d])
        if d != order[3]:
            send(sa.at[1, 1, low], sa.at[0, 1, low], sa_s, sa_r.at[2, d], near3)
        send(sa.at[1, 1, rows], sa.at[1, 0, rows], sp_s, sp_r.at[1, d], partner)
        wait(sa.at[2, 1, rows], sa_r.at[1, d])
        if d != order[3]:
            send(sa.at[2, 1, high], sa.at[0, 1, high], sa_s, sa_r.at[3, d], near1)
        send(sa.at[2, 1, rows], sa.at[2, 0, rows], sp_s, sp_r.at[2, d], partner)

    def opposite(d):
        rows = rows_of(d)
        if d == order[3]:
            wait(sa.at[0, 1, rows], sa_r.at[2, d])
        else:
            wait(sa.at[0, 1, rows_of(d, 0, 32)], sa_r.at[2, d])
            wait(sa.at[0, 1, rows_of(d, 32, 32)], sa_r.at[3, d])
        send(sa.at[0, 1, rows], sa.at[0, 0, rows], sp_s, sp_r.at[0, d], partner)

    d0, d1, d2, d3 = order
    side_s(d0)
    pass_on(d0)
    side_s(d1)
    opposite(d0)
    pass_on(d1)
    side_s(d2)
    opposite(d1)
    pass_on(d2)
    side_s(d3)
    opposite(d2)
    wait(ai_v, ld_ai)
    acc = jnp.dot(ai_v[3, 1], sa[3, 1], preferred_element_type=F32)
    pass_on(d3)
    acc += jnp.dot(ai_v[1, 1], sa[1, 1], preferred_element_type=F32)
    opposite(d3)
    acc += jnp.dot(ai_v[2, 1], sa[2, 1], preferred_element_type=F32)
    acc += jnp.dot(ai_v[0, 1], sa[0, 1], preferred_element_type=F32)
    for k in (3, 1, 2, 0):
        for d in range(4):
            wait(sa.at[k, 0, rows_of(d)], sp_r.at[k, d])
        acc += jnp.dot(ai_v[k, 0], sa[k, 0], preferred_element_type=F32)

    for j in range(4):
        xs[j] = acc[:, j * 128 : (j + 1) * 128].astype(BF16).reshape(ZL, 16, 128)
    for j in range(4):
        xx = lax.rem(x + j, XS)

        def send_solved(i, carry, xx=xx):
            zz = lax.rem(zl + off8(i), ZL)
            send(xs.at[xx, zz], rx.at[lay], x_s, x_r, at(xx * ZL + zz, y, zh, c))
            return carry

        lax.fori_loop(0, 7 if j == 0 else 8, send_solved, 0)
    pltpu.make_async_copy(xs.at[x, zl], rx.at[lay], x_r).start()

    wait(rx, x_r)
    state = None
    for l in range(LAYERS):
        solved = rx[l].astype(F32)
        state = solved if state is None else solved + cpl[l - 1] * state
        dd[l] = state.astype(BF16)

    for j in range(4):
        xx = lax.rem(x + j, XS)

        def send_lower(i, carry, xx=xx):
            zz = lax.rem(zl + off8(i), ZL)
            ll = xx * ZL + zz
            send(dd.at[ll], ot.at[zl, x], d_s, d_r, at(ll, y, zh, c))
            return carry

        lax.fori_loop(0, 7 if j == 0 else 8, send_lower, 0)
    pltpu.make_async_copy(dd.at[lay], ot.at[zl, x], d_r).start()

    wait(ot, d_r)
    for j in range(XS):
        out[0, :, j * 128 : (j + 1) * 128] = ot[:, j].reshape(ROWS, 128)

    wait(pr, pair_s)
    wait(so, y_s)
    wait(sd, y_s)
    wait(sf, y_s)
    wait(dks.at[pl.ds(0, LAYERS - 1)], dk_s)
    wait(r.at[pl.ds(0, 2 * LAYERS - 1)], r_s)
    for d in order:
        wait(u.at[pl.ds(0, 15 if d == 0 else 16)], u_s.at[d])
    wait(sa.at[pl.ds(0, 1), 0], sa_s)
    wait(sa.at[pl.ds(0, 1), 0], sa_s)
    wait(sa.at[pl.ds(0, 1), 0], sa_s)
    wait(sa.at[:, 0], sp_s)
    wait(rx.at[pl.ds(0, LAYERS - 1)], x_s)
    wait(rx.at[pl.ds(0, LAYERS - 1)], d_s)


def shards(activations, out_grads, a_inverse, s_inverse, in_decay, out_decay):
    vm = pltpu.VMEM
    dma = pltpu.SemaphoreType.DMA
    outside = pl.BlockSpec(memory_space=pltpu.HBM)
    inside = pl.BlockSpec(memory_space=pltpu.VMEM)
    unit = (4, 2, 128, 128)
    scratch = [
        vm((TOK, DIN), BF16),
        vm((TOK, DOUT), BF16),
        vm((DOUT, TOK), BF16),
        vm((4, 2, ROWS, 256), BF16),
        vm((DOUT, DOUT), BF16),
        vm((1, ROWS), F32),
        vm((1, DOUT), F32),
        vm((2, 4, 4, 2, 128, 128), F32),
        vm((4, 4, 2, 128, 128), F32),
        vm(unit, BF16), vm(unit, BF16), vm(unit, F32),
        vm(unit, BF16), vm(unit, BF16), vm(unit, F32),
        vm((4, 2, ZL, 16, 128), BF16),
        vm((2 * LAYERS, 16, 128), BF16),
        vm((XS, 2, 128), F32),
        vm((LAYERS, 2, 128), F32),
        vm((128, 128), F32),
        vm((LAYERS, 16, 128), F32),
        vm((LAYERS, 16, 128), BF16),
        vm((ZS, XS, 16, 128), BF16),
        vm((4, 2, 256, DOUT), BF16),
        vm((4, ZL, 16, 128), BF16),
        vm((LAYERS, 16, 128), BF16),
        vm((LAYERS, 16, 128), BF16),
        vm((ZL, XS, 16, 128), BF16),
        dma(()), dma(()), dma(()), dma(()), dma((2,)),
        pltpu.SemaphoreType.REGULAR((4,)),
        dma(()), dma((4,)),
        dma(()), dma((4, 2)), dma((4, 2)), dma((4, 2)),
        dma(()), dma(()),
        dma(()), dma(()),
        dma((4,)), dma((4,)),
        dma(()), dma((4, 4)),
        dma(()), dma((4, 4)),
        dma(()), dma(()),
        dma(()), dma(()),
    ]
    return pl.pallas_call(
        kernel,
        out_shape=jax.ShapeDtypeStruct((1, ROWS, DOUT), BF16),
        in_specs=[outside] * 6,
        out_specs=inside,
        scratch_shapes=scratch,
        compiler_params=pltpu.CompilerParams(
            collective_id=0, has_side_effects=True, vmem_limit_bytes=67043328
        ),
    )(activations, out_grads, a_inverse, s_inverse, in_decay, out_decay)


def solution(mesh):
    placed = (
        P("layer", "dp", None),
        P("layer", "dp", None),
        P("layer", "dp", None),
        P("layer", None, None),
        P("layer", "dp"),
        P("layer", None),
    )
    return jax.shard_map(
        shards, mesh=mesh, in_specs=placed, out_specs=P("layer", "dp", None), check_vma=False
    )
```

time: 92.3 us -> 89.5 us (0.970)
  Pallas kernels: 90.6 us -> 87.2 us
    pallas_call x1, Pallas kernels: 90.6 us -> 87.2 us  [shards(): pl.pallas_call(kernel, out_shape=jax.ShapeDtypeStruct((1, ROWS, DOUT), BF...]
where the time goes in v3:
time: 89.5 us; the launch traced here: 88.8 us
  Pallas kernels  87.2 us (97%)
  local copies, waits for them, and re-layouts  1.57 us (2%)
    pallas_call x1, Pallas kernels, shards(): pl.pallas_call(kernel, out_shape=jax.ShapeDtypeStruct((1, ROWS, DOUT), BF...  87.2 us

profile of v3, /device:TPU:6, one launch (start us, length us, event | category | flops | bytes accessed | tf_op | source)
XLA Modules:
  0.0 88.8 jit_solution(5234733454590073218)
XLA Ops:
  0.0 87.2 %shard_map.64 = bf16[1,128,512]{2,1,0:T(8,128)(2,1)} custom-call(bf16[1,640,2048]{2,1,0:T(8,128)(2,1)} %acts.1, bf16[1,640,512]{2,1,0:T(8,128)(2,1)} %og.1, bf16[1,128,2048]{2,1,0:T(8,128)(2,1)} %ainv.1, bf16[1,512,512]{2,1,0:T(8,128)(2,1)} %sinv.1, f32[1,128]{1,0:T(1,128)} %ind.1, f32[1,512]{1,0:T(1,128)} %outd.1), custom_call_target="tpu_custom_call" | custom-call | tf_op jit(solution)/shard_map/pallas_call | solution.py:383
  87.2 1.6 %copy.8 = bf16[1,128,512]{2,1,0:T(8,128)(2,1)} copy(bf16[1,128,512]{2,1,0:T(8,128)(2,1)} %shard_map.64) | data formatting | bytes 262144
